TPU v7x, 32 devices: a whole 2x2x4 slice. The times are simulated.
32 devices in a mesh: dp: 4 (over z), rows: 4 (over y, core), cols: 2 (over x).
Axes of the slice: x: 2, y: 2, z: 4, core: 2. Of those that a mesh axis runs over, the one named last changes fastest.
Arguments:
- hidden_in: bfloat16 [3072, 1536], P(('dp', 'cols'), 'rows'), may hold values from -7 to 7
- attn_gain: float32 [2, 1536], P(None, 'rows'), may hold values from 0.1 to 1.9
- w_qkv: bfloat16 [2, 1536, 2048], P(None, 'rows', 'cols'), may hold values from -0.15625 to 0.15625
- b_qkv: float32 [2, 2048], P(None, 'cols'), may hold values from -2 to 2
- w_out: bfloat16 [2, 1536, 1536], P(None, 'cols', 'rows'), may hold values from -0.3125 to 0.3125
- mlp_gain: float32 [2, 1536], P(None, 'rows'), may hold values from 0.1 to 1.9
- w_gate: bfloat16 [2, 1536, 8960], P(None, 'rows', 'cols'), may hold values from -0.15625 to 0.15625
- w_up: bfloat16 [2, 1536, 8960], P(None, 'rows', 'cols'), may hold values from -0.15625 to 0.15625
- w_down: bfloat16 [2, 8960, 1536], P(None, 'cols', 'rows'), may hold values from -0.0625 to 0.0625
- out_grad: bfloat16 [3072, 1536], P(('dp', 'cols'), 'rows'), may hold values from -6 to 6
Outputs:
- hidden_out: bfloat16 [3072, 1536], P(('dp', 'cols'), 'rows')
- in_grad: float32 [3072, 1536], P(('dp', 'cols'), 'rows')
- attn_gain_grad: float32 [2, 1536], P(None, 'rows')
- w_qkv_grad: float32 [2, 1536, 2048], P(None, 'rows', 'cols')
- b_qkv_grad: float32 [2, 2048], P(None, 'cols')
- w_out_grad: float32 [2, 1536, 1536], P(None, 'cols', 'rows')
- mlp_gain_grad: float32 [2, 1536], P(None, 'rows')
- w_gate_grad: float32 [2, 1536, 8960], P(None, 'rows', 'cols')
- w_up_grad: float32 [2, 1536, 8960], P(None, 'rows', 'cols')
- w_down_grad: float32 [2, 8960, 1536], P(None, 'cols', 'rows')
All inputs are finite; a program needn't handle non-finite values.
Results may differ from a plain program's by a relative error of at most 0.025.
Values may be sent and summed in bfloat16 or wider, within the bound.
No kernel may reach another device: no remote copies, remote signals or barrier semaphores. Data moves between devices by JAX's collectives and lax.ppermute only.
A program may use at most 320 MiB of HBM per device.

v0:
```python
import jax
import jax.numpy as jnp
from jax import lax
from jax.sharding import PartitionSpec as P

D = 1536
HEADS = 12
KV_HEADS = 2
HEAD_DIM = 128
SEQ = 192
LAYERS = 2
QKV = 2048
eps = 1e-06
theta = 1000000.0
masked = -1e30


def rotate_half(values):
    half_dim = values.shape[-1] // 2
    return jnp.concatenate([-values[..., half_dim:], values[..., :half_dim]], axis=-1)


def rope_tables():
    frequency = theta ** (-jnp.arange(0, HEAD_DIM, 2, dtype=jnp.float32) / HEAD_DIM)
    angles = jnp.arange(SEQ, dtype=jnp.float32)[:, None] * frequency[None, :]
    angles = jnp.concatenate([angles, angles], axis=-1)
    return (jnp.cos(angles), jnp.sin(angles))


def causal_scores(query_round, key_round):
    raw_scores = jnp.einsum(
        "sikgd,sjkd->skgij", query_round, key_round, preferred_element_type=jnp.float32
    ) * HEAD_DIM ** (-0.5)
    position = jnp.arange(SEQ)
    return jnp.where(position[:, None] >= position[None, :], raw_scores, masked)


def attention_forward(qkv_rows, kv_count, group_size):
    blocks = qkv_rows.reshape(-1, SEQ, kv_count, group_size + 2, HEAD_DIM)
    cosine, sine_table = rope_tables()
    query = blocks[:, :, :, :group_size]
    key_part = blocks[:, :, :, group_size]
    value_part = blocks[:, :, :, group_size + 1]
    query = (
        query * cosine[None, :, None, None, :]
        + rotate_half(query) * sine_table[None, :, None, None, :]
    )
    key_part = (
        key_part * cosine[None, :, None, :] + rotate_half(key_part) * sine_table[None, :, None, :]
    )
    query_round = query.astype(jnp.bfloat16)
    key_round = key_part.astype(jnp.bfloat16)
    value_round = value_part.astype(jnp.bfloat16)
    scores = causal_scores(query_round, key_round)
    highest = jnp.max(scores, axis=-1, keepdims=True)
    log_total = highest + jnp.log(jnp.sum(jnp.exp(scores - highest), axis=-1, keepdims=True))
    weights_round = jnp.exp(scores - log_total).astype(jnp.bfloat16)
    attended = jnp.einsum(
        "skgij,sjkd->sikgd", weights_round, value_round, preferred_element_type=jnp.float32
    )
    attended = attended.astype(jnp.bfloat16).reshape(qkv_rows.shape[0], -1)
    return (attended, (query_round, key_round, value_round, log_total))


def attention_backward(grad_attended, attn_kept, kv_count, group_size):
    query_round, key_round, value_round, log_total = attn_kept
    grad_round = grad_attended.astype(jnp.bfloat16).reshape(-1, SEQ, kv_count, group_size, HEAD_DIM)
    scores = causal_scores(query_round, key_round)
    prob_full = jnp.exp(scores - log_total)
    weights_round = prob_full.astype(jnp.bfloat16)
    grad_value = jnp.einsum(
        "skgij,sikgd->sjkd", weights_round, grad_round, preferred_element_type=jnp.float32
    )
    grad_prob = jnp.einsum(
        "sikgd,sjkd->skgij", grad_round, value_round, preferred_element_type=jnp.float32
    )
    grad_scores = (
        prob_full
        * (grad_prob - jnp.sum(prob_full * grad_prob, axis=-1, keepdims=True))
        * HEAD_DIM ** (-0.5)
    )
    grad_scores = grad_scores.astype(jnp.bfloat16)
    grad_query = jnp.einsum(
        "skgij,sjkd->sikgd", grad_scores, key_round, preferred_element_type=jnp.float32
    )
    grad_key = jnp.einsum(
        "skgij,sikgd->sjkd", grad_scores, query_round, preferred_element_type=jnp.float32
    )
    cosine, sine_table = rope_tables()
    grad_query = (
        grad_query * cosine[None, :, None, None, :]
        - rotate_half(grad_query) * sine_table[None, :, None, None, :]
    )
    grad_key = (
        grad_key * cosine[None, :, None, :] - rotate_half(grad_key) * sine_table[None, :, None, :]
    )
    joined = jnp.concatenate(
        [grad_query, grad_key[:, :, :, None], grad_value[:, :, :, None]], axis=3
    )
    return joined.reshape(grad_attended.shape[0], -1)


def norm_forward(resid, gain_row):
    squares = jnp.sum(resid * resid, axis=1)
    totals = lax.psum(squares, "rows")
    scale_row = lax.rsqrt(totals / D + eps)
    normed = (resid * scale_row[:, None] * gain_row[None, :]).astype(jnp.bfloat16)
    return (normed, scale_row)


def norm_backward(grad_normed, resid, scale_row, gain_row):
    scaled = grad_normed * gain_row[None, :]
    inner = lax.psum(jnp.sum(scaled * resid, axis=1), "rows")
    gain_grad = jnp.sum(grad_normed * resid * scale_row[:, None], axis=0)
    grad_resid = (
        scale_row[:, None] * scaled
        - resid * (scale_row * scale_row * scale_row * inner / D)[:, None]
    )
    return (grad_resid, gain_grad)


def gather_cols(values):
    return lax.all_gather(values, "cols", axis=0, tiled=True)


def gather_rows(values):
    return lax.all_gather(values, "rows", axis=0, tiled=True)


def widen(gathered, weight):
    per_device = gathered.shape[0] // lax.axis_size("rows")

    def partial_term(first_row, length_rows):
        return jnp.dot(gathered, weight, preferred_element_type=jnp.float32)

    return lax.psum_scatter(
        partial_term(jnp.int32(0), lax.axis_size("rows") * per_device),
        "rows",
        scatter_dimension=0,
        tiled=True,
    )


def narrow(gathered, weight):
    per_device = gathered.shape[0] // lax.axis_size("cols")

    def partial_term(first_row, length_rows):
        return jnp.dot(gathered, weight, preferred_element_type=jnp.float32)

    return lax.psum_scatter(
        partial_term(jnp.int32(0), per_device * lax.axis_size("cols")).astype(jnp.bfloat16),
        "cols",
        scatter_dimension=0,
        tiled=True,
    ).astype(jnp.float32)


def back_narrow(grad_resid, weight):
    grad_round = grad_resid.astype(jnp.bfloat16)
    gathered = lax.all_gather(grad_round, "cols", axis=0, tiled=True)
    per_device = gathered.shape[0] // lax.axis_size("rows")

    def partial_term(first_row, length_rows):
        return lax.dot_general(
            gathered, weight, (((1,), (1,)), ((), ())), preferred_element_type=jnp.float32
        )

    return (
        lax.psum_scatter(
            partial_term(jnp.int32(0), per_device * lax.axis_size("rows")).astype(jnp.bfloat16),
            "rows",
            scatter_dimension=0,
            tiled=True,
        ).astype(jnp.float32),
        gathered,
    )


def back_widen(grad_round, weight):
    gathered = lax.all_gather(grad_round, "rows", axis=0, tiled=True)
    per_device = gathered.shape[0] // lax.axis_size("cols")

    def partial_term(first_row, length_rows):
        return lax.dot_general(
            gathered, weight, (((1,), (1,)), ((), ())), preferred_element_type=jnp.float32
        )

    return (
        lax.psum_scatter(
            partial_term(jnp.int32(0), per_device * lax.axis_size("cols")).astype(jnp.bfloat16),
            "cols",
            scatter_dimension=0,
            tiled=True,
        ).astype(jnp.float32),
        gathered,
    )


def weight_grad(left_rows, right_rows):
    return lax.dot_general(
        left_rows, right_rows, (((0,), (0,)), ((), ())), preferred_element_type=jnp.float32
    )


def spread(first_grad, second_grad, third_grad, fourth_grad, fifth_grad):
    summed = (
        lax.psum_scatter(
            first_grad.astype(jnp.bfloat16), "dp", scatter_dimension=1, tiled=True
        ).astype(jnp.float32),
        lax.psum_scatter(
            second_grad.astype(jnp.bfloat16), "dp", scatter_dimension=1, tiled=True
        ).astype(jnp.float32),
        lax.psum_scatter(
            third_grad.astype(jnp.bfloat16), "dp", scatter_dimension=1, tiled=True
        ).astype(jnp.float32),
        lax.psum_scatter(
            fourth_grad.astype(jnp.bfloat16), "dp", scatter_dimension=1, tiled=True
        ).astype(jnp.float32),
        lax.psum_scatter(
            fifth_grad.astype(jnp.bfloat16), "dp", scatter_dimension=1, tiled=True
        ).astype(jnp.float32),
    )
    return (
        lax.all_gather(summed[0].astype(jnp.bfloat16), "dp", axis=1, tiled=True).astype(
            jnp.float32
        ),
        lax.all_gather(summed[1].astype(jnp.bfloat16), "dp", axis=1, tiled=True).astype(
            jnp.float32
        ),
        lax.all_gather(summed[2].astype(jnp.bfloat16), "dp", axis=1, tiled=True).astype(
            jnp.float32
        ),
        lax.all_gather(summed[3].astype(jnp.bfloat16), "dp", axis=1, tiled=True).astype(
            jnp.float32
        ),
        lax.all_gather(summed[4].astype(jnp.bfloat16), "dp", axis=1, tiled=True).astype(
            jnp.float32
        ),
    )


def body(hidden_in, attn_gain, w_qkv, b_qkv, w_out, mlp_gain, w_gate, w_up, w_down, out_grad):
    kv_count = KV_HEADS // lax.axis_size("cols")
    group_size = HEADS // KV_HEADS
    hidden_units = w_gate.shape[2]
    resid = hidden_in.astype(jnp.float32)
    saved = []
    for which_layer in range(LAYERS):
        normed_attn, scale_attn = norm_forward(resid, attn_gain[which_layer])
        gathered_attn = gather_cols(normed_attn)
        qkv_rows = widen(gathered_attn, w_qkv[which_layer]) + b_qkv[which_layer][None, :]
        attended, attn_kept = attention_forward(qkv_rows, kv_count, group_size)
        gathered_heads = gather_rows(attended)
        middle = resid + narrow(gathered_heads, w_out[which_layer])
        normed_mlp, scale_mlp = norm_forward(middle, mlp_gain[which_layer])
        gathered_mlp = gather_cols(normed_mlp)
        joined = jnp.concatenate([w_gate[which_layer], w_up[which_layer]], axis=1)
        both_proj = widen(gathered_mlp, joined)
        gate_proj = both_proj[:, :hidden_units]
        up_proj = both_proj[:, hidden_units:]
        activated = (jax.nn.silu(gate_proj) * up_proj).astype(jnp.bfloat16)
        gathered_units = gather_rows(activated)
        store = (gathered_attn, gathered_heads, gathered_mlp, gathered_units)
        saved.append((resid, scale_attn, attn_kept, middle, scale_mlp, gate_proj, up_proj, store))
        resid = middle + narrow(gathered_units, w_down[which_layer])
    hidden_out = resid.astype(jnp.bfloat16)
    grad_resid = out_grad.astype(jnp.float32)
    layer_grads = [None] * LAYERS
    attn_gain_parts = [None] * LAYERS
    mlp_gain_parts = [None] * LAYERS
    bias_parts = [None] * LAYERS
    for which_layer in reversed(range(LAYERS)):
        resid, scale_attn, attn_kept, middle, scale_mlp, gate_proj, up_proj, store = saved[
            which_layer
        ]
        rows_attn, rows_heads, rows_mlp, rows_units = store
        grad_units, down_gathered = back_narrow(grad_resid, w_down[which_layer])
        down_grad = weight_grad(rows_units, down_gathered)
        sigmoid_gate = jax.nn.sigmoid(gate_proj)
        grad_gate = grad_units * up_proj * sigmoid_gate * (1.0 + gate_proj * (1.0 - sigmoid_gate))
        grad_up = grad_units * gate_proj * sigmoid_gate
        grad_both = jnp.concatenate(
            [grad_gate.astype(jnp.bfloat16), grad_up.astype(jnp.bfloat16)], axis=1
        )
        joined = jnp.concatenate([w_gate[which_layer], w_up[which_layer]], axis=1)
        grad_normed_mlp, both_gathered = back_widen(grad_both, joined)
        both_grad = weight_grad(rows_mlp, both_gathered)
        grad_inner, mlp_gain_part = norm_backward(
            grad_normed_mlp, middle, scale_mlp, mlp_gain[which_layer]
        )
        grad_middle = grad_resid + grad_inner
        grad_heads, heads_gathered = back_narrow(grad_middle, w_out[which_layer])
        out_weight_grad = weight_grad(rows_heads, heads_gathered)
        grad_qkv = attention_backward(grad_heads, attn_kept, kv_count, group_size)
        bias_part = jnp.sum(grad_qkv, axis=0)
        grad_normed_attn, qkv_gathered = back_widen(
            grad_qkv.astype(jnp.bfloat16), w_qkv[which_layer]
        )
        qkv_weight_grad = weight_grad(rows_attn, qkv_gathered)
        grad_first, attn_gain_part = norm_backward(
            grad_normed_attn, resid, scale_attn, attn_gain[which_layer]
        )
        grad_resid = grad_middle + grad_first
        attn_gain_parts[which_layer] = attn_gain_part
        mlp_gain_parts[which_layer] = mlp_gain_part
        bias_parts[which_layer] = bias_part
        grads_now = (
            qkv_weight_grad,
            out_weight_grad,
            both_grad[:, :hidden_units],
            both_grad[:, hidden_units:],
            down_grad,
        )
        layer_grads[which_layer] = grads_now
    stacked = [
        jnp.stack([layer_grads[which_layer][member] for which_layer in range(LAYERS)])
        for member in range(5)
    ]
    merged = spread(stacked[0], stacked[1], stacked[2], stacked[3], stacked[4])
    row_width = attn_gain.shape[1]
    col_width = b_qkv.shape[1]
    row_place = lax.axis_index("rows") * row_width
    col_place = lax.axis_index("cols") * col_width
    attn_full = lax.dynamic_update_slice(
        jnp.zeros((LAYERS, D), jnp.float32), jnp.stack(attn_gain_parts), (0, row_place)
    )
    mlp_full = lax.dynamic_update_slice(
        jnp.zeros((LAYERS, D), jnp.float32), jnp.stack(mlp_gain_parts), (0, row_place)
    )
    bias_full = lax.dynamic_update_slice(
        jnp.zeros((LAYERS, QKV), jnp.float32), jnp.stack(bias_parts), (0, col_place)
    )
    totals = lax.psum((attn_full, mlp_full, bias_full), ("dp", "rows", "cols"))
    attn_gain_grad = lax.dynamic_slice_in_dim(totals[0], row_place, row_width, 1)
    mlp_gain_grad = lax.dynamic_slice_in_dim(totals[1], row_place, row_width, 1)
    bias_grad = lax.dynamic_slice_in_dim(totals[2], col_place, col_width, 1)
    return (
        hidden_out,
        grad_resid,
        attn_gain_grad,
        merged[0],
        bias_grad,
        merged[1],
        mlp_gain_grad,
        merged[2],
        merged[3],
        merged[4],
    )


def solution(mesh):
    in_specs = (
        P(("dp", "cols"), "rows"),
        P(None, "rows"),
        P(None, "rows", "cols"),
        P(None, "cols"),
        P(None, "cols", "rows"),
        P(None, "rows"),
        P(None, "rows", "cols"),
        P(None, "rows", "cols"),
        P(None, "cols", "rows"),
        P(("dp", "cols"), "rows"),
    )
    out_specs = (
        P(("dp", "cols"), "rows"),
        P(("dp", "cols"), "rows"),
        P(None, "rows"),
        P(None, "rows", "cols"),
        P(None, "cols"),
        P(None, "cols", "rows"),
        P(None, "rows"),
        P(None, "rows", "cols"),
        P(None, "rows", "cols"),
        P(None, "cols", "rows"),
    )
    return jax.shard_map(body, mesh=mesh, in_specs=in_specs, out_specs=out_specs, check_vma=False)
```

profile of v0, /device:TPU:0, one launch (start us, length us, event | category | flops | bytes accessed | tf_op | source)
XLA Modules:
  0.0 2279.8 jit_solution(14332408452359226671)
XLA Ops:
  32.6 38.2 %reduce-scatter.22.cloned.1.call-done = f32[192,1024]{1,0:T(8,128)} async-done(((f32[768,1024]{1,0:T(8,128)}), f32[192,1024]{1,0:T(8,128)}) %reduce-scatter.22.cloned.1.call-update) | async-done | bytes 786448 | tf_op jit(solution)/shard_map/reduce_scatter | solution.py:136
  146.7 197.8 %reduce-scatter.26.cloned.1.call-done = f32[192,8960]{1,0:T(8,128)} async-done(((f32[768,8960]{1,0:T(8,128)}), f32[192,8960]{1,0:T(8,128)}) %reduce-scatter.26.cloned.1.call-update) | async-done | bytes 6881296 | tf_op jit(solution)/shard_map/reduce_scatter | solution.py:136
  350.2 49.3 %all-gather.16.cloned.1.call-done = bf16[768,4480]{1,0:T(8,128)(2,1)} async-done(((bf16[192,4480]{1,0:T(8,128)(2,1)}), bf16[768,4480]{1,0:T(8,128)(2,1)}) %all-gather.16.cloned.1.call-update) | async-done | bytes 6881296 | tf_op jit(solution)/shard_map/all_gather | solution.py:127
  444.1 38.0 %reduce-scatter.30.cloned.1.call-done = f32[192,1024]{1,0:T(8,128)} async-done(((f32[768,1024]{1,0:T(8,128)}), f32[192,1024]{1,0:T(8,128)}) %reduce-scatter.30.cloned.1.call-update) | async-done | bytes 786448 | tf_op jit(solution)/shard_map/reduce_scatter | solution.py:136
  487.9 17.5 all-gather.18.cloned.1.call-done
  568.4 25.3 %reduce-scatter.38.cloned.1.call-done = bf16[192,4480]{1,0:T(8,128)(2,1)} async-done(((bf16[768,4480]{1,0:T(8,128)(2,1)}), bf16[192,4480]{1,0:T(8,128)(2,1)}) %reduce-scatter.38.cloned.1.call-update) | async-done | bytes 1720336 | tf_op jit(solution)/shard_map/reduce_scatter | solution.py:169
  593.7 200.3 %reduce-scatter.34.cloned.1.call-done = f32[192,8960]{1,0:T(8,128)} async-done(((f32[768,8960]{1,0:T(8,128)}), f32[192,8960]{1,0:T(8,128)}) %reduce-scatter.34.cloned.1.call-update) | async-done | bytes 6881296 | tf_op jit(solution)/shard_map/reduce_scatter | solution.py:136
  801.5 88.9 %all-gather.22.cloned.1.call-done = bf16[768,8960]{1,0:T(8,128)(2,1)} async-done(((bf16[192,8960]{1,0:T(8,128)(2,1)}), bf16[768,8960]{1,0:T(8,128)(2,1)}) %all-gather.22.cloned.1.call-update) | async-done | bytes 13762576 | tf_op jit(solution)/shard_map/all_gather | solution.py:180
  943.3 25.7 %reduce-scatter.42.cloned.1.call-done = bf16[192,768]{1,0:T(8,128)(2,1)} async-done(((bf16[768,768]{1,0:T(8,128)(2,1)}), bf16[192,768]{1,0:T(8,128)(2,1)}) %reduce-scatter.42.cloned.1.call-update) | async-done | bytes 294928 | tf_op jit(solution)/shard_map/reduce_scatter | solution.py:169
  974.8 19.2 all-gather.24.cloned.1.call-done
  997.7 47.9 %all-gather.20.cloned.1.call-done = bf16[768,4480]{1,0:T(8,128)(2,1)} async-done(((bf16[192,4480]{1,0:T(8,128)(2,1)}), bf16[768,4480]{1,0:T(8,128)(2,1)}) %all-gather.20.cloned.1.call-update) | async-done | bytes 6881296 | tf_op jit(solution)/shard_map/all_gather | solution.py:127
  1102.0 63.0 %reduce-scatter.46.cloned.1.call-done = bf16[192,4480]{1,0:T(8,128)(2,1)} async-done(((bf16[768,4480]{1,0:T(8,128)(2,1)}), bf16[192,4480]{1,0:T(8,128)(2,1)}) %reduce-scatter.46.cloned.1.call-update) | async-done | bytes 1720336 | tf_op jit(solution)/shard_map/reduce_scatter | solution.py:169
  1171.4 88.9 %all-gather.26.cloned.1.call-done = bf16[768,8960]{1,0:T(8,128)(2,1)} async-done(((bf16[192,8960]{1,0:T(8,128)(2,1)}), bf16[768,8960]{1,0:T(8,128)(2,1)}) %all-gather.26.cloned.1.call-update) | async-done | bytes 13762576 | tf_op jit(solution)/shard_map/all_gather | solution.py:180
  1311.1 25.3 %reduce-scatter.50.cloned.1.call-done = bf16[192,768]{1,0:T(8,128)(2,1)} async-done(((bf16[768,768]{1,0:T(8,128)(2,1)}), bf16[192,768]{1,0:T(8,128)(2,1)}) %reduce-scatter.50.cloned.1.call-update) | async-done | bytes 294928 | tf_op jit(solution)/shard_map/reduce_scatter | solution.py:169
  1410.7 73.6 %reduce-scatter.62.cloned.1.call-done = bf16[2,1120,384]{2,1,0:T(8,128)(2,1)} async-done(((bf16[2,4480,384]{2,1,0:T(8,128)(2,1)}), bf16[2,1120,384]{2,1,0:T(8,128)(2,1)}) %reduce-scatter.62.cloned.1.call-update) | async-done | bytes 1720336 | tf_op jit(solution)/shard_map/reduce_scatter | solution.py:219
  1484.4 32.7 %reduce-scatter.56.cloned.1.call-done = bf16[2,192,384]{2,1,0:T(8,128)(2,1)} async-done(((bf16[2,768,384]{2,1,0:T(8,128)(2,1)}), bf16[2,192,384]{2,1,0:T(8,128)(2,1)}) %reduce-scatter.56.cloned.1.call-update) | async-done | bytes 294928 | tf_op jit(solution)/shard_map/reduce_scatter | solution.py:210
  1520.8 33.1 %reduce-scatter.54.cloned.1.call-done = bf16[2,96,1024]{2,1,0:T(8,128)(2,1)} async-done(((bf16[2,384,1024]{2,1,0:T(8,128)(2,1)}), bf16[2,96,1024]{2,1,0:T(8,128)(2,1)}) %reduce-scatter.54.cloned.1.call-update) | async-done | bytes 393232 | tf_op jit(solution)/shard_map/reduce_scatter | solution.py:207
  1554.0 121.9 %reduce-scatter.58.cloned.1.call-done = bf16[2,96,4480]{2,1,0:T(8,128)(2,1)} async-done(((bf16[2,384,4480]{2,1,0:T(8,128)(2,1)}), bf16[2,96,4480]{2,1,0:T(8,128)(2,1)}) %reduce-scatter.58.cloned.1.call-update) | async-done | bytes 1720336 | tf_op jit(solution)/shard_map/reduce_scatter | solution.py:213
  1676.1 123.5 %reduce-scatter.60.cloned.1.call-done = bf16[2,96,4480]{2,1,0:T(8,128)(2,1)} async-done(((bf16[2,384,4480]{2,1,0:T(8,128)(2,1)}), bf16[2,96,4480]{2,1,0:T(8,128)(2,1)}) %reduce-scatter.60.cloned.1.call-update) | async-done | bytes 1720336 | tf_op jit(solution)/shard_map/reduce_scatter | solution.py:216
  1799.8 126.9 %all-gather.38.cloned.1.call-done = bf16[2,4480,384]{2,1,0:T(8,128)(2,1)} async-done(((bf16[2,1120,384]{2,1,0:T(8,128)(2,1)}), bf16[2,4480,384]{2,1,0:T(8,128)(2,1)}) %all-gather.38.cloned.1.call-update) | async-done | bytes 6881296 | tf_op jit(solution)/shard_map/all_gather | solution.py:236
  1935.9 20.7 all-gather.32.cloned.1.call-done
  1981.7 41.7 %all-reduce = (f32[2,1536]{1,0:T(2,128)S(1)}, f32[2,2048]{1,0:T(2,128)S(1)}, f32[2,1536]{1,0:T(2,128)S(1)}) all-reduce(f32[2,1536]{1,0:T(2,128)S(1)} %maximum_dynamic-update-slice_fusion.1, f32[2,2048]{1,0:T(2,128)S(1)} %maximum_dynamic-update-slice_fusion, ...), channel_id=1, replica_groups=mesh['dp'=4,'rows'=4,'cols'=2] {'dp','rows','cols'}, use_global_device_ids=true, to_apply=%region_40.41 | all-reduce | flops 10240 | bytes 81920 | tf_op jit(solution)/shard_map/psum | solution.py:333
  2030.9 108.1 %all-gather.34.cloned.1.call-done = bf16[2,384,4480]{2,1,0:T(8,128)(2,1)} async-done(((bf16[2,96,4480]{2,1,0:T(8,128)(2,1)}), bf16[2,384,4480]{2,1,0:T(8,128)(2,1)}) %all-gather.34.cloned.1.call-update) | async-done | bytes 6881296 | tf_op jit(solution)/shard_map/all_gather | solution.py:230
  2148.6 115.2 %all-gather.36.cloned.1.call-done = bf16[2,384,4480]{2,1,0:T(8,128)(2,1)} async-done(((bf16[2,96,4480]{2,1,0:T(8,128)(2,1)}), bf16[2,384,4480]{2,1,0:T(8,128)(2,1)}) %all-gather.36.cloned.1.call-update) | async-done | bytes 6881296 | tf_op jit(solution)/shard_map/all_gather | solution.py:233
  (413 shorter events, 540.8 us)
Async XLA Ops:
  97.0 247.5 %reduce-scatter.26.cloned.1.call-start = ((), (), s32[]{:S(2)}) async-start(), calls=%async_computation.24 | async-start | bytes 34406400 | tf_op jit(solution)/shard_map/reduce_scatter | solution.py:136
  146.6 252.9 %all-gather.16.cloned.1.call-start = ((), (), s32[]{:S(2)}) async-start(), calls=%async_computation.25 | async-start | bytes 8601600 | tf_op jit(solution)/shard_map/all_gather | solution.py:127
  349.7 73.9 %reduce-scatter.28.cloned.1.call-start = ((), (), s32[]{:S(2)}) async-start(), calls=%async_computation.26 | async-start | bytes 884736 | tf_op jit(solution)/shard_map/reduce_scatter | solution.py:150
  408.1 74.0 %reduce-scatter.30.cloned.1.call-start = ((), (), s32[]{:S(2)}) async-start(), calls=%async_computation.27 | async-start | bytes 3932160 | tf_op jit(solution)/shard_map/reduce_scatter | solution.py:136
  508.5 85.3 %reduce-scatter.38.cloned.1.call-start = ((), (), s32[]{:S(2)}) async-start(), calls=%async_computation.33 | async-start | bytes 8601600 | tf_op jit(solution)/shard_map/reduce_scatter | solution.py:169
  530.1 264.0 %reduce-scatter.34.cloned.1.call-start = ((), (), s32[]{:S(2)}) async-start(), calls=%async_computation.30 | async-start | bytes 34406400 | tf_op jit(solution)/shard_map/reduce_scatter | solution.py:136
  568.4 322.0 %all-gather.22.cloned.1.call-start = ((), (), s32[]{:S(2)}) async-start(), calls=%async_computation.34 | async-start | bytes 17203200 | tf_op jit(solution)/shard_map/all_gather | solution.py:180
  801.4 117.7 %reduce-scatter.40.cloned.1.call-start = ((), (), s32[]{:S(2)}) async-start(), calls=%async_computation.35 | async-start | bytes 884736 | tf_op jit(solution)/shard_map/reduce_scatter | solution.py:189
  974.7 89.0 %reduce-scatter.44.cloned.1.call-start = ((), (), s32[]{:S(2)}) async-start(), calls=%async_computation.38 | async-start | bytes 884736 | tf_op jit(solution)/shard_map/reduce_scatter | solution.py:189
  997.5 84.3 %reduce-scatter.36.cloned.1.call-start = ((), (), s32[]{:S(2)}) async-start(), calls=%async_computation.32 | async-start | bytes 884736 | tf_op jit(solution)/shard_map/reduce_scatter | solution.py:150
  1054.2 110.8 %reduce-scatter.46.cloned.1.call-start = ((), (), s32[]{:S(2)}) async-start(), calls=%async_computation.39 | async-start | bytes 8601600 | tf_op jit(solution)/shard_map/reduce_scatter | solution.py:169
  1101.9 158.3 %all-gather.26.cloned.1.call-start = ((), (), s32[]{:S(2)}) async-start(), calls=%async_computation.40 | async-start | bytes 17203200 | tf_op jit(solution)/shard_map/all_gather | solution.py:180
  1171.3 117.5 %reduce-scatter.48.cloned.1.call-start = ((), (), s32[]{:S(2)}) async-start(), calls=%async_computation.41 | async-start | bytes 884736 | tf_op jit(solution)/shard_map/reduce_scatter | solution.py:189
  1341.4 142.9 %reduce-scatter.62.cloned.1.call-start = ((), (), s32[]{:S(2)}) async-start(), calls=%async_computation.53 | async-start | bytes 8601600 | tf_op jit(solution)/shard_map/reduce_scatter | solution.py:219
  1359.0 158.1 %reduce-scatter.56.cloned.1.call-start = ((), (), s32[]{:S(2)}) async-start(), calls=%async_computation.47 | async-start | bytes 1474560 | tf_op jit(solution)/shard_map/reduce_scatter | solution.py:210
  1365.5 188.4 %reduce-scatter.54.cloned.1.call-start = ((), (), s32[]{:S(2)}) async-start(), calls=%async_computation.45 | async-start | bytes 1966080 | tf_op jit(solution)/shard_map/reduce_scatter | solution.py:207
  1386.0 289.8 %reduce-scatter.58.cloned.1.call-start = ((), (), s32[]{:S(2)}) async-start(), calls=%async_computation.49 | async-start | bytes 8601600 | tf_op jit(solution)/shard_map/reduce_scatter | solution.py:213
  1404.0 395.6 %reduce-scatter.60.cloned.1.call-start = ((), (), s32[]{:S(2)}) async-start(), calls=%async_computation.51 | async-start | bytes 8601600 | tf_op jit(solution)/shard_map/reduce_scatter | solution.py:216
  1410.6 516.1 %all-gather.38.cloned.1.call-start = ((), (), s32[]{:S(2)}) async-start(), calls=%async_computation.54 | async-start | bytes 8601600 | tf_op jit(solution)/shard_map/all_gather | solution.py:236
  1484.3 472.3 %all-gather.32.cloned.1.call-start = ((), (), s32[]{:S(2)}) async-start(), calls=%async_computation.48 | async-start | bytes 1474560 | tf_op jit(solution)/shard_map/all_gather | solution.py:227
  1517.2 456.9 %reduce-scatter.52.cloned.1.call-start = ((), (), s32[]{:S(2)}) async-start(), calls=%async_computation.44 | async-start | bytes 884736 | tf_op jit(solution)/shard_map/reduce_scatter | solution.py:189
  1520.7 506.7 %all-gather.30.cloned.1.call-start = ((), (), s32[]{:S(2)}) async-start(), calls=%async_computation.46 | async-start | bytes 1966080 | tf_op jit(solution)/shard_map/all_gather | solution.py:224
  1553.9 585.1 %all-gather.34.cloned.1.call-start = ((), (), s32[]{:S(2)}) async-start(), calls=%async_computation.50 | async-start | bytes 8601600 | tf_op jit(solution)/shard_map/all_gather | solution.py:230
  1675.9 587.9 %all-gather.36.cloned.1.call-start = ((), (), s32[]{:S(2)}) async-start(), calls=%async_computation.52 | async-start | bytes 8601600 | tf_op jit(solution)/shard_map/all_gather | solution.py:233
  (96 other events, 5503.2 us)
Sparse Core Ops, SparseCore 0:
  31.5 39.2 reduce-scatter.21
  146.7 197.7 reduce-scatter.25
  349.8 49.6 all-gather.15
  444.2 37.9 reduce-scatter.29
  530.2 63.5 reduce-scatter.37
  596.4 197.6 reduce-scatter.33
  801.6 88.7 all-gather.21
  943.4 25.5 reduce-scatter.41
  974.3 19.6 all-gather.23
  995.9 49.6 all-gather.19
  1102.0 62.8 reduce-scatter.45
  1171.4 88.7 all-gather.25
  1310.8 25.5 reduce-scatter.49
  1341.5 19.6 all-gather.27
  1363.9 120.3 reduce-scatter.61
  1487.2 29.8 reduce-scatter.55
  1519.8 34.0 reduce-scatter.53
  1556.6 119.1 reduce-scatter.57
  1678.7 120.8 reduce-scatter.59
  1801.2 125.4 all-gather.37
  1928.1 28.4 all-gather.31
  1975.6 38.0 all-gather.29
  2015.1 123.8 all-gather.33
  2140.5 123.1 all-gather.35
  (10 shorter events, 158.3 us)
where the time goes:
time: 2290 us; the launch traced here: 2280 us
  waiting for transfers between devices  1780 us (78%)
  blocking collectives  171 us (7%)
  matrix products  170 us (7%)
  other arithmetic  102 us (4%)
  local copies, waits for them, and re-layouts  34.1 us (1%)
    reduce_scatter x4, waiting for transfers between devices, widen(): lax.psum_scatter(partial_term(jnp.int32(0), lax.axis_size('rows') * per_d...  474 us
    all_gather x4, waiting for transfers between devices, back_widen(): gathered = lax.all_gather(grad_round, 'rows', axis=0, tiled=True)  197 us
    reduce_scatter x4, waiting for transfers between devices, back_narrow(): lax.psum_scatter(partial_term(jnp.int32(0), per_device * lax.axis_size('r...  139 us
    all_gather x4, waiting for transfers between devices, gather_rows(): return lax.all_gather(values, 'rows', axis=0, tiled=True)  132 us
    all_gather x1, waiting for transfers between devices, spread(): lax.all_gather(summed[4].astype(jnp.bfloat16), 'dp', axis=1, tiled=True)  127 us
    reduce_scatter x1, waiting for transfers between devices, spread(): lax.psum_scatter(fourth_grad.astype(jnp.bfloat16), 'dp', scatter_dimensio...  123 us
    reduce_scatter x1, waiting for transfers between devices, spread(): lax.psum_scatter(third_grad.astype(jnp.bfloat16), 'dp', scatter_dimension...  122 us
    all_gather x1, waiting for transfers between devices, spread(): lax.all_gather(summed[3].astype(jnp.bfloat16), 'dp', axis=1, tiled=True)  115 us
  transfers between devices with their start and end apart: 34, of which 31 were waited for; matrix products, arithmetic and copies ran while one was open for 7% of the time, Pallas kernels for 0%

commit v1 on v0

--- a/solution.py
+++ b/solution.py
@@ -15,6 +15,31 @@
 masked = -1e30
 
 
+def name_field(piece_in, dim_i):
+    row_out = list(piece_in.shape[1:])
+    row_out[dim_i] *= piece_in.shape[0]
+    return jnp.moveaxis(piece_in, 0, dim_i).reshape(row_out)
+
+
+def cut_turns(chunk, mesh_ax):
+    world_n = lax.axis_size(mesh_ax)
+    carry_in = chunk[None]
+    for it in range(world_n.bit_length() - 1):
+        frame_out = 1 << it
+        odd = lax.ppermute(
+            carry_in, axis_name=mesh_ax, perm=[(ix, ix ^ frame_out) for ix in range(world_n)]
+        )
+        tall = jnp.stack([carry_in, odd], axis=0)
+        fresh = lax.axis_index(mesh_ax) >> it & 1
+        carry_in = jnp.where(fresh == 0, tall, tall[::-1]).reshape(-1, *chunk.shape)
+    return carry_in
+
+
+def _close_hubs(xin, u, where_dim):
+    state_next = cut_turns(xin, u)
+    return name_field(state_next, where_dim)
+
+
 def rotate_half(values):
     half_dim = values.shape[-1] // 2
     return jnp.concatenate([-values[..., half_dim:], values[..., :half_dim]], axis=-1)
@@ -227,9 +252,7 @@
         lax.all_gather(summed[1].astype(jnp.bfloat16), "dp", axis=1, tiled=True).astype(
             jnp.float32
         ),
-        lax.all_gather(summed[2].astype(jnp.bfloat16), "dp", axis=1, tiled=True).astype(
-            jnp.float32
-        ),
+        _close_hubs(summed[2].astype(jnp.bfloat16), "dp", 1).astype(jnp.float32),
         lax.all_gather(summed[3].astype(jnp.bfloat16), "dp", axis=1, tiled=True).astype(
             jnp.float32
         ),

time: 2290 us -> 2320 us (1.013)
    all_gather x1, waiting for transfers between devices: 127 us -> 241 us  [spread(): lax.all_gather(summed[4].astype(jnp.bfloat16), 'dp', axis=1, tiled=True)]
    all_gather x1 -> x0, waiting for transfers between devices: 108 us -> none  [spread(): lax.all_gather(summed[2].astype(jnp.bfloat16), 'dp', axis=1, tiled=True)]
    all_gather x1, waiting for transfers between devices: 115 us -> 77 us  [spread(): lax.all_gather(summed[3].astype(jnp.bfloat16), 'dp', axis=1, tiled=True)]
    reduce_scatter x1, waiting for transfers between devices: 123 us -> 150 us  [spread(): lax.psum_scatter(fourth_grad.astype(jnp.bfloat16), 'dp', scatter_dimensio...]
  transfers between devices with their start and end apart: 34 -> 35, of which waited for: 31 -> 30; matrix products, arithmetic and copies ran while one was open for 7% -> 8% of each run, Pallas kernels for 0% -> 0%
where the time goes in v1:
time: 2320 us
  waiting for transfers between devices  1790 us (77%)
  blocking collectives  171 us (7%)
  matrix products  170 us (7%)
  other arithmetic  118 us (5%)
  local copies, waits for them, and re-layouts  45.2 us (2%)
    reduce_scatter x4, waiting for transfers between devices, widen(): lax.psum_scatter(partial_term(jnp.int32(0), lax.axis_size('rows') * per_d...  474 us
    all_gather x1, waiting for transfers between devices, spread(): lax.all_gather(summed[4].astype(jnp.bfloat16), 'dp', axis=1, tiled=True)  241 us
    all_gather x4, waiting for transfers between devices, back_widen(): gathered = lax.all_gather(grad_round, 'rows', axis=0, tiled=True)  197 us
    reduce_scatter x1, waiting for transfers between devices, spread(): lax.psum_scatter(fourth_grad.astype(jnp.bfloat16), 'dp', scatter_dimensio...  150 us
    reduce_scatter x4, waiting for transfers between devices, back_narrow(): lax.psum_scatter(partial_term(jnp.int32(0), per_device * lax.axis_size('r...  139 us
    all_gather x4, waiting for transfers between devices, gather_rows(): return lax.all_gather(values, 'rows', axis=0, tiled=True)  132 us
    reduce_scatter x1, waiting for transfers between devices, spread(): lax.psum_scatter(third_grad.astype(jnp.bfloat16), 'dp', scatter_dimension...  122 us
    all_gather x1, waiting for transfers between devices, spread(): lax.all_gather(summed[3].astype(jnp.bfloat16), 'dp', axis=1, tiled=True)  77 us
  transfers between devices with their start and end apart: 35, of which 30 were waited for; matrix products, arithmetic and copies ran while one was open for 8% of the time, Pallas kernels for 0%

profile of v1, /device:TPU:0, one launch (start us, length us, event | category | flops | bytes accessed | tf_op | source)
XLA Modules:
  0.0 2315.1 jit_solution(5945569344935593002)
XLA Ops:
  32.6 38.2 %reduce-scatter.22.cloned.1.call-done = f32[192,1024]{1,0:T(8,128)} async-done(((f32[768,1024]{1,0:T(8,128)}), f32[192,1024]{1,0:T(8,128)}) %reduce-scatter.22.cloned.1.call-update) | async-done | bytes 786448 | tf_op jit(solution)/shard_map/reduce_scatter | solution.py:161
  146.7 197.8 %reduce-scatter.26.cloned.1.call-done = f32[192,8960]{1,0:T(8,128)} async-done(((f32[768,8960]{1,0:T(8,128)}), f32[192,8960]{1,0:T(8,128)}) %reduce-scatter.26.cloned.1.call-update) | async-done | bytes 6881296 | tf_op jit(solution)/shard_map/reduce_scatter | solution.py:161
  350.2 49.3 %all-gather.15.cloned.1.call-done = bf16[768,4480]{1,0:T(8,128)(2,1)} async-done(((bf16[192,4480]{1,0:T(8,128)(2,1)}), bf16[768,4480]{1,0:T(8,128)(2,1)}) %all-gather.15.cloned.1.call-update) | async-done | bytes 6881296 | tf_op jit(solution)/shard_map/all_gather | solution.py:152
  444.1 38.0 %reduce-scatter.30.cloned.1.call-done = f32[192,1024]{1,0:T(8,128)} async-done(((f32[768,1024]{1,0:T(8,128)}), f32[192,1024]{1,0:T(8,128)}) %reduce-scatter.30.cloned.1.call-update) | async-done | bytes 786448 | tf_op jit(solution)/shard_map/reduce_scatter | solution.py:161
  487.9 17.5 all-gather.17.cloned.1.call-done
  551.2 17.1 fusion.3
  568.4 25.3 %reduce-scatter.38.cloned.1.call-done = bf16[192,4480]{1,0:T(8,128)(2,1)} async-done(((bf16[768,4480]{1,0:T(8,128)(2,1)}), bf16[192,4480]{1,0:T(8,128)(2,1)}) %reduce-scatter.38.cloned.1.call-update) | async-done | bytes 1720336 | tf_op jit(solution)/shard_map/reduce_scatter | solution.py:194
  593.7 200.3 %reduce-scatter.34.cloned.1.call-done = f32[192,8960]{1,0:T(8,128)} async-done(((f32[768,8960]{1,0:T(8,128)}), f32[192,8960]{1,0:T(8,128)}) %reduce-scatter.34.cloned.1.call-update) | async-done | bytes 6881296 | tf_op jit(solution)/shard_map/reduce_scatter | solution.py:161
  801.5 88.9 %all-gather.21.cloned.1.call-done = bf16[768,8960]{1,0:T(8,128)(2,1)} async-done(((bf16[192,8960]{1,0:T(8,128)(2,1)}), bf16[768,8960]{1,0:T(8,128)(2,1)}) %all-gather.21.cloned.1.call-update) | async-done | bytes 13762576 | tf_op jit(solution)/shard_map/all_gather | solution.py:205
  943.3 25.7 %reduce-scatter.42.cloned.1.call-done = bf16[192,768]{1,0:T(8,128)(2,1)} async-done(((bf16[768,768]{1,0:T(8,128)(2,1)}), bf16[192,768]{1,0:T(8,128)(2,1)}) %reduce-scatter.42.cloned.1.call-update) | async-done | bytes 294928 | tf_op jit(solution)/shard_map/reduce_scatter | solution.py:194
  974.8 19.2 all-gather.23.cloned.1.call-done
  997.7 47.9 %all-gather.19.cloned.1.call-done = bf16[768,4480]{1,0:T(8,128)(2,1)} async-done(((bf16[192,4480]{1,0:T(8,128)(2,1)}), bf16[768,4480]{1,0:T(8,128)(2,1)}) %all-gather.19.cloned.1.call-update) | async-done | bytes 6881296 | tf_op jit(solution)/shard_map/all_gather | solution.py:152
  1102.0 63.0 %reduce-scatter.46.cloned.1.call-done = bf16[192,4480]{1,0:T(8,128)(2,1)} async-done(((bf16[768,4480]{1,0:T(8,128)(2,1)}), bf16[192,4480]{1,0:T(8,128)(2,1)}) %reduce-scatter.46.cloned.1.call-update) | async-done | bytes 1720336 | tf_op jit(solution)/shard_map/reduce_scatter | solution.py:194
  1171.4 88.9 %all-gather.25.cloned.1.call-done = bf16[768,8960]{1,0:T(8,128)(2,1)} async-done(((bf16[192,8960]{1,0:T(8,128)(2,1)}), bf16[768,8960]{1,0:T(8,128)(2,1)}) %all-gather.25.cloned.1.call-update) | async-done | bytes 13762576 | tf_op jit(solution)/shard_map/all_gather | solution.py:205
  1311.1 25.3 %reduce-scatter.50.cloned.1.call-done = bf16[192,768]{1,0:T(8,128)(2,1)} async-done(((bf16[768,768]{1,0:T(8,128)(2,1)}), bf16[192,768]{1,0:T(8,128)(2,1)}) %reduce-scatter.50.cloned.1.call-update) | async-done | bytes 294928 | tf_op jit(solution)/shard_map/reduce_scatter | solution.py:194
  1410.7 73.6 %reduce-scatter.62.cloned.1.call-done = bf16[2,1120,384]{2,1,0:T(8,128)(2,1)} async-done(((bf16[2,4480,384]{2,1,0:T(8,128)(2,1)}), bf16[2,1120,384]{2,1,0:T(8,128)(2,1)}) %reduce-scatter.62.cloned.1.call-update) | async-done | bytes 1720336 | tf_op jit(solution)/shard_map/reduce_scatter | solution.py:244
  1484.4 32.7 %reduce-scatter.56.cloned.1.call-done = bf16[2,192,384]{2,1,0:T(8,128)(2,1)} async-done(((bf16[2,768,384]{2,1,0:T(8,128)(2,1)}), bf16[2,192,384]{2,1,0:T(8,128)(2,1)}) %reduce-scatter.56.cloned.1.call-update) | async-done | bytes 294928 | tf_op jit(solution)/shard_map/reduce_scatter | solution.py:235
  1520.7 33.2 %reduce-scatter.54.cloned.1.call-done = bf16[2,96,1024]{2,1,0:T(8,128)(2,1)} async-done(((bf16[2,384,1024]{2,1,0:T(8,128)(2,1)}), bf16[2,96,1024]{2,1,0:T(8,128)(2,1)}) %reduce-scatter.54.cloned.1.call-update) | async-done | bytes 393232 | tf_op jit(solution)/shard_map/reduce_scatter | solution.py:232
  1554.2 121.7 %reduce-scatter.58.cloned.1.call-done = bf16[2,96,4480]{2,1,0:T(8,128)(2,1)} async-done(((bf16[2,384,4480]{2,1,0:T(8,128)(2,1)}), bf16[2,96,4480]{2,1,0:T(8,128)(2,1)}) %reduce-scatter.58.cloned.1.call-update) | async-done | bytes 1720336 | tf_op jit(solution)/shard_map/reduce_scatter | solution.py:238
  1677.3 150.3 %reduce-scatter.60.cloned.1.call-done = bf16[2,96,4480]{2,1,0:T(8,128)(2,1)} async-done(((bf16[2,384,4480]{2,1,0:T(8,128)(2,1)}), bf16[2,96,4480]{2,1,0:T(8,128)(2,1)}) %reduce-scatter.60.cloned.1.call-update) | async-done | bytes 1720336 | tf_op jit(solution)/shard_map/reduce_scatter | solution.py:241
  1837.1 241.2 %all-gather.35.cloned.1.call-done = bf16[2,4480,384]{2,1,0:T(8,128)(2,1)} async-done(((bf16[2,1120,384]{2,1,0:T(8,128)(2,1)}), bf16[2,4480,384]{2,1,0:T(8,128)(2,1)}) %all-gather.35.cloned.1.call-update) | async-done | bytes 6881296 | tf_op jit(solution)/shard_map/all_gather | solution.py:259
  2087.6 28.0 %all-gather.31.cloned.1.call-done = bf16[2,768,384]{2,1,0:T(8,128)(2,1)} async-done(((bf16[2,192,384]{2,1,0:T(8,128)(2,1)}), bf16[2,768,384]{2,1,0:T(8,128)(2,1)}) %all-gather.31.cloned.1.call-update) | async-done | bytes 1179664 | tf_op jit(solution)/shard_map/all_gather | solution.py:252
  2141.8 41.7 %all-reduce = (f32[2,1536]{1,0:T(2,128)S(1)}, f32[2,2048]{1,0:T(2,128)S(1)}, f32[2,1536]{1,0:T(2,128)S(1)}) all-reduce(f32[2,1536]{1,0:T(2,128)S(1)} %maximum_dynamic-update-slice_fusion.1, f32[2,2048]{1,0:T(2,128)S(1)} %maximum_dynamic-update-slice_fusion, ...), channel_id=1, replica_groups=mesh['dp'=4,'rows'=4,'cols'=2] {'dp','rows','cols'}, use_global_device_ids=true, to_apply=%region_40.41 | all-reduce | flops 10240 | bytes 81920 | tf_op jit(solution)/shard_map/psum | solution.py:356
  2222.0 77.0 %all-gather.33.cloned.1.call-done = bf16[2,384,4480]{2,1,0:T(8,128)(2,1)} async-done(((bf16[2,96,4480]{2,1,0:T(8,128)(2,1)}), bf16[2,384,4480]{2,1,0:T(8,128)(2,1)}) %all-gather.33.cloned.1.call-update) | async-done | bytes 6881296 | tf_op jit(solution)/shard_map/all_gather | solution.py:256
  (419 shorter events, 556.8 us)
Async XLA Ops:
  97.0 247.5 %reduce-scatter.26.cloned.1.call-start = ((), (), s32[]{:S(2)}) async-start(), calls=%async_computation.24 | async-start | bytes 34406400 | tf_op jit(solution)/shard_map/reduce_scatter | solution.py:161
  146.6 252.9 %all-gather.15.cloned.1.call-start = ((), (), s32[]{:S(2)}) async-start(), calls=%async_computation.25 | async-start | bytes 8601600 | tf_op jit(solution)/shard_map/all_gather | solution.py:152
  408.1 74.0 %reduce-scatter.30.cloned.1.call-start = ((), (), s32[]{:S(2)}) async-start(), calls=%async_computation.27 | async-start | bytes 3932160 | tf_op jit(solution)/shard_map/reduce_scatter | solution.py:161
  508.5 85.3 %reduce-scatter.38.cloned.1.call-start = ((), (), s32[]{:S(2)}) async-start(), calls=%async_computation.33 | async-start | bytes 8601600 | tf_op jit(solution)/shard_map/reduce_scatter | solution.py:194
  530.1 264.0 %reduce-scatter.34.cloned.1.call-start = ((), (), s32[]{:S(2)}) async-start(), calls=%async_computation.30 | async-start | bytes 34406400 | tf_op jit(solution)/shard_map/reduce_scatter | solution.py:161
  568.4 322.0 %all-gather.21.cloned.1.call-start = ((), (), s32[]{:S(2)}) async-start(), calls=%async_computation.34 | async-start | bytes 17203200 | tf_op jit(solution)/shard_map/all_gather | solution.py:205
  801.4 117.7 %reduce-scatter.40.cloned.1.call-start = ((), (), s32[]{:S(2)}) async-start(), calls=%async_computation.35 | async-start | bytes 884736 | tf_op jit(solution)/shard_map/reduce_scatter | solution.py:214
  974.7 89.0 %reduce-scatter.44.cloned.1.call-start = ((), (), s32[]{:S(2)}) async-start(), calls=%async_computation.38 | async-start | bytes 884736 | tf_op jit(solution)/shard_map/reduce_scatter | solution.py:214
  997.5 84.3 %reduce-scatter.36.cloned.1.call-start = ((), (), s32[]{:S(2)}) async-start(), calls=%async_computation.32 | async-start | bytes 884736 | tf_op jit(solution)/shard_map/reduce_scatter | solution.py:175
  1054.2 110.8 %reduce-scatter.46.cloned.1.call-start = ((), (), s32[]{:S(2)}) async-start(), calls=%async_computation.39 | async-start | bytes 8601600 | tf_op jit(solution)/shard_map/reduce_scatter | solution.py:194
  1101.9 158.3 %all-gather.25.cloned.1.call-start = ((), (), s32[]{:S(2)}) async-start(), calls=%async_computation.40 | async-start | bytes 17203200 | tf_op jit(solution)/shard_map/all_gather | solution.py:205
  1171.3 117.5 %reduce-scatter.48.cloned.1.call-start = ((), (), s32[]{:S(2)}) async-start(), calls=%async_computation.41 | async-start | bytes 884736 | tf_op jit(solution)/shard_map/reduce_scatter | solution.py:214
  1341.4 142.9 %reduce-scatter.62.cloned.1.call-start = ((), (), s32[]{:S(2)}) async-start(), calls=%async_computation.52 | async-start | bytes 8601600 | tf_op jit(solution)/shard_map/reduce_scatter | solution.py:244
  1359.0 158.1 %reduce-scatter.56.cloned.1.call-start = ((), (), s32[]{:S(2)}) async-start(), calls=%async_computation.47 | async-start | bytes 1474560 | tf_op jit(solution)/shard_map/reduce_scatter | solution.py:235
  1365.5 188.4 %reduce-scatter.54.cloned.1.call-start = ((), (), s32[]{:S(2)}) async-start(), calls=%async_computation.45 | async-start | bytes 1966080 | tf_op jit(solution)/shard_map/reduce_scatter | solution.py:232
  1386.0 289.8 %reduce-scatter.58.cloned.1.call-start = ((), (), s32[]{:S(2)}) async-start(), calls=%async_computation.49 | async-start | bytes 8601600 | tf_op jit(solution)/shard_map/reduce_scatter | solution.py:238
  1404.0 423.7 %reduce-scatter.60.cloned.1.call-start = ((), (), s32[]{:S(2)}) async-start(), calls=%async_computation.50 | async-start | bytes 8601600 | tf_op jit(solution)/shard_map/reduce_scatter | solution.py:241
  1410.6 667.8 %all-gather.35.cloned.1.call-start = ((), (), s32[]{:S(2)}) async-start(), calls=%async_computation.53 | async-start | bytes 8601600 | tf_op jit(solution)/shard_map/all_gather | solution.py:259
  1484.3 631.3 %all-gather.31.cloned.1.call-start = ((), (), s32[]{:S(2)}) async-start(), calls=%async_computation.48 | async-start | bytes 1474560 | tf_op jit(solution)/shard_map/all_gather | solution.py:252
  1517.1 617.0 %reduce-scatter.52.cloned.1.call-start = ((), (), s32[]{:S(2)}) async-start(), calls=%async_computation.44 | async-start | bytes 884736 | tf_op jit(solution)/shard_map/reduce_scatter | solution.py:214
  1520.6 666.9 %all-gather.29.cloned.1.call-start = ((), (), s32[]{:S(2)}) async-start(), calls=%async_computation.46 | async-start | bytes 1966080 | tf_op jit(solution)/shard_map/all_gather | solution.py:249
  1553.9 745.1 %all-gather.33.cloned.1.call-start = ((), (), s32[]{:S(2)}) async-start(), calls=%async_computation.51 | async-start | bytes 8601600 | tf_op jit(solution)/shard_map/all_gather | solution.py:256
  1675.8 151.9 %collective-permute-start = (bf16[1,2,96,4480]{3,2,1,0:T(8,128)(2,1)}, bf16[1,2,96,4480]{3,2,1,0:T(8,128)(2,1)}, u32[]{:S(2)}, u32[]{:S(2)}) collective-permute-start(bf16[1,2,96,4480]{3,2,1,0:T(8,128)(2,1)} %bitcast.329), channel_id=1, source_target_pairs={{0,8},{8,0},{16,24},{24,16},{1,9},{9,1},{17,25},{25,17},{2,10},{10... | collective-permute-start | bytes 5160968 | tf_op jit(solution)/shard_map/ppermute | solution.py:29
  1833.6 357.3 %collective-permute-start.1 = (bf16[2,2,96,4480]{3,2,1,0:T(8,128)(2,1)}, bf16[2,2,96,4480]{3,2,1,0:T(8,128)(2,1)}, u32[]{:S(2)}, u32[]{:S(2)}) collective-permute-start(bf16[2,2,96,4480]{3,2,1,0:T(8,128)(2,1)} %get-tuple-element.43), channel_id=1, source_target_pairs={{0,16},{8,24},{16,0},{24,8},{1,17},{9,25},{17,1},{25,9},{2,18},{10... | collective-permute-start | bytes 10321928 | tf_op jit(solution)/shard_map/ppermute | solution.py:29
  (97 other events, 4587.8 us)
Sparse Core Ops, SparseCore 0:
  31.5 39.2 reduce-scatter.21
  146.7 197.7 reduce-scatter.25
  349.8 49.6 all-gather.14
  444.2 37.9 reduce-scatter.29
  488.0 17.4 all-gather.16
  530.2 63.5 reduce-scatter.37
  596.4 197.6 reduce-scatter.33
  801.6 88.7 all-gather.20
  943.4 25.5 reduce-scatter.41
  974.3 19.6 all-gather.22
  995.9 49.6 all-gather.18
  1102.0 62.8 reduce-scatter.45
  1171.4 88.7 all-gather.24
  1310.8 25.5 reduce-scatter.49
  1341.5 19.6 all-gather.26
  1363.9 120.3 reduce-scatter.61
  1487.2 29.8 reduce-scatter.55
  1519.8 34.0 reduce-scatter.53
  1556.6 119.1 reduce-scatter.57
  1678.7 148.9 reduce-scatter.59
  1829.2 249.0 all-gather.34
  2079.8 35.7 all-gather.30
  2135.7 37.9 all-gather.28
  2175.1 123.8 all-gather.32
  (9 shorter events, 141.9 us)
